TPU v7x, 32 devices: a whole 2x2x4 slice. The times are simulated.
32 devices in a mesh: dp: 32 (over z, y, x, core), tensor: 1.
Axes of the slice: x: 2, y: 2, z: 4, core: 2. Of those that a mesh axis runs over, the one named last changes fastest.
Arguments:
- tokens: bfloat16 [8192, 2048], P('dp', 'tensor'), may hold values from -6 to 6
- expert_ids: int32 [8192, 2], P('dp'), may hold values from 0 to 31, as said below
- route_weights: float32 [8192, 2], P('dp'), may hold values from 0.2 to 1
- gate_weight: bfloat16 [32, 2048, 1024], P('dp', None, 'tensor'), may hold values from -0.125 to 0.125
- up_weight: bfloat16 [32, 2048, 1024], P('dp', None, 'tensor'), may hold values from -0.125 to 0.125
- down_weight: bfloat16 [32, 1024, 2048], P('dp', 'tensor'), may hold values from -0.1875 to 0.1875
Outputs:
- moe_out: bfloat16 [8192, 2048], P('dp', 'tensor')
Inputs may be any that keep to these rules, and one draw needn't show every extreme that they name: `expert_ids`: the two experts of a row differ. Among the rows of one index of dp, no expert is named more than 32 times.
All inputs are finite; a program needn't handle non-finite values.
Results may differ from a plain program's by a relative error of at most 0.011.
Values may be sent and summed in bfloat16 or wider, within the bound.
No kernel may reach another device: no remote copies, remote signals or barrier semaphores. Data moves between devices by JAX's collectives and lax.ppermute only.
A program may use at most 64 MiB of HBM per device.

v0:
```python
import functools

import jax
import jax.numpy as jnp
from jax import lax
from jax.experimental import pallas as pl
from jax.experimental.pallas import tpu as pltpu
from jax.sharding import PartitionSpec as P


MIB = 1024 * 1024
F32 = jnp.float32
BF16 = jnp.bfloat16
CHUNKS = 2


def plan_kernel(experts, capacity, me_ref, ids_ref, weights_ref, pick_ref, high_ref, low_ref):
    ids, route = ids_ref[...], weights_ref[...]
    tokens = ids.shape[1]
    names = jnp.bitwise_xor(
        me_ref[0], lax.broadcasted_iota(jnp.int32, (experts, tokens), 0)
    ).astype(ids.dtype)
    first = ids[0:1, :] == names
    second = ids[1:2, :] == names
    named = jnp.where(first, 1.0, 0.0) + jnp.where(second, 1.0, 0.0)
    weight = jnp.where(first, route[0:1, :], 0.0) + jnp.where(second, route[1:2, :], 0.0)
    earlier = jnp.where(
        lax.broadcasted_iota(jnp.int32, (tokens, tokens), 0)
        < lax.broadcasted_iota(jnp.int32, (tokens, tokens), 1),
        1.0,
        0.0,
    )
    rank = jnp.dot(named.astype(BF16), earlier.astype(BF16), preferred_element_type=F32)
    rank = jnp.where(named > 0.5, rank, -1.0).astype(jnp.int32)
    slot = lax.broadcasted_iota(jnp.int32, (experts, capacity, tokens), 1)
    mask = rank[:, None, :] == slot
    slots = experts * capacity
    pick_ref[...] = jnp.where(mask, 1.0, 0.0).reshape(slots, tokens).astype(BF16)
    spread = jnp.where(mask, weight[:, None, :], 0.0).reshape(slots, tokens).T
    high = spread.astype(BF16)
    high_ref[...] = high
    low_ref[...] = (spread - high.astype(F32)).astype(BF16)


def make_plan(me, ids, route, blocks, capacity):
    tokens = ids.shape[1]
    slots = 2 * blocks * capacity
    vmem = pl.BlockSpec(memory_space=pltpu.VMEM)
    return pl.pallas_call(
        functools.partial(plan_kernel, 2 * blocks, capacity),
        out_shape=[
            jax.ShapeDtypeStruct((slots, tokens), BF16),
            jax.ShapeDtypeStruct((tokens, slots), BF16),
            jax.ShapeDtypeStruct((tokens, slots), BF16),
        ],
        in_specs=[pl.BlockSpec(memory_space=pltpu.SMEM), vmem, vmem],
        out_specs=[vmem] * 3,
        compiler_params=pltpu.CompilerParams(vmem_limit_bytes=6 * MIB),
        cost_estimate=pl.CostEstimate(
            flops=40 * slots * tokens, bytes_accessed=6 * slots * tokens, transcendentals=0
        ),
        name="plan",
    )(me, ids, route)


def dispatch_kernel(blocks, pick_ref, tokens_ref, *refs):
    outs, rest = refs[:blocks], refs[blocks:]
    width = tokens_ref.shape[1]
    rows = outs[0].shape[0]
    for i, copy in enumerate(rest):
        step = copy.shape[1]
        copy[...] = tokens_ref[:, i * step : (i + 1) * step]
    tile = min(width, 512)
    for col in range(0, width, tile):
        picked = jnp.dot(pick_ref[...], tokens_ref[:, col : col + tile], preferred_element_type=F32)
        picked = picked.astype(BF16)
        for k, out in enumerate(outs):
            out[:, col : col + tile] = picked[k * rows : (k + 1) * rows]


def dispatch(plan, tokens, blocks, rest=0):
    pick = plan[0]
    slots = pick.shape[0]
    width = tokens.shape[1]
    vmem = pl.BlockSpec(memory_space=pltpu.VMEM)
    return pl.pallas_call(
        functools.partial(dispatch_kernel, blocks),
        out_shape=[jax.ShapeDtypeStruct((slots // blocks, width), BF16)] * blocks
        + [jax.ShapeDtypeStruct((tokens.shape[0], width // max(rest, 1)), BF16)] * rest,
        in_specs=[vmem, vmem],
        out_specs=[vmem] * (blocks + rest),
        compiler_params=pltpu.CompilerParams(vmem_limit_bytes=8 * MIB),
        cost_estimate=pl.CostEstimate(
            flops=2 * slots * tokens.shape[0] * width,
            bytes_accessed=2 * slots * width + 2 * tokens.size,
            transcendentals=0,
        ),
        name="dispatch",
    )(pick, tokens)


def mix_kernel(blocks, high_ref, low_ref, *refs):
    parts = refs[:blocks]
    out, held, sems = refs[blocks:]
    rows = parts[0].shape[0]
    copies = [
        pltpu.make_async_copy(part, held.at[pl.ds(k * rows, rows)], sems.at[k])
        for k, part in enumerate(parts)
    ]
    for copy in copies:
        copy.start()
    for copy in copies:
        copy.wait()
    width = held.shape[1]
    tile = min(width, 512)
    for col in range(0, width, tile):
        rows_here = held[:, col : col + tile]
        mixed = jnp.dot(high_ref[...], rows_here, preferred_element_type=F32)
        mixed += jnp.dot(low_ref[...], rows_here, preferred_element_type=F32)
        out[:, col : col + tile] = mixed.astype(out.dtype)


def mix(plan, parts, dtype):
    blocks = len(parts)
    _, width = parts[0].shape
    _, high, low = plan
    tokens, slots = high.shape
    vmem = pl.BlockSpec(memory_space=pltpu.VMEM)
    return pl.pallas_call(
        functools.partial(mix_kernel, blocks),
        out_shape=jax.ShapeDtypeStruct((tokens, width), dtype),
        in_specs=[vmem, vmem] + [pl.BlockSpec(memory_space=pl.ANY)] * blocks,
        out_specs=vmem,
        scratch_shapes=[
            pltpu.VMEM((slots, width), BF16),
            pltpu.SemaphoreType.DMA((blocks,)),
        ],
        compiler_params=pltpu.CompilerParams(vmem_limit_bytes=8 * MIB),
        cost_estimate=pl.CostEstimate(
            flops=4 * slots * tokens * width,
            bytes_accessed=2 * slots * width + 4 * tokens * width,
            transcendentals=0,
        ),
        name="mix",
    )(high, low, *parts)


def experts_kernel(blocks, capacity, widths, first, *refs):
    pieces = blocks * len(widths)
    refs = list(refs)

    def take(n):
        taken = refs[:n]
        del refs[:n]
        return taken

    parts, gates, ups = take(pieces), take(2), take(2)
    downs = take(2) if first else None
    outs = take(blocks) if first else []
    hidden, rows_in, gate, up, part_sems, gate_sems, up_sems = take(7)
    down, down_sems = refs if first else (None, None)
    tile = gate.shape[2] // gate_sems.shape[1]
    down_tiles = down_sems.shape[1] if first else 0
    down_tile = first // max(down_tiles, 1)
    offsets = [sum(widths[:i]) for i in range(len(widths))]

    def part_copy(e, n):
        chunk, k = divmod(n, blocks)
        return pltpu.make_async_copy(
            parts[n].at[pl.ds(e * capacity, capacity)],
            rows_in.at[e, pl.ds(k * capacity, capacity), pl.ds(offsets[chunk], widths[chunk])],
            part_sems.at[e, n],
        )

    def weight_copy(source, target, sems, e, i, size):
        columns = pl.ds(i * size, size)
        return pltpu.make_async_copy(
            source[e].at[0, :, columns], target.at[e, :, columns], sems.at[e, i]
        )

    for e in range(2):
        for n in range(pieces):
            part_copy(e, n).start()
        for i in range(gate_sems.shape[1]):
            weight_copy(gates, gate, gate_sems, e, i, tile).start()
            weight_copy(ups, up, up_sems, e, i, tile).start()
    for e in range(2):
        for i in range(down_tiles):
            weight_copy(downs, down, down_sems, e, i, down_tile).start()
    for e in range(2):
        for n in range(pieces):
            part_copy(e, n).wait()
        for i in range(gate_sems.shape[1]):
            weight_copy(gates, gate, gate_sems, e, i, tile).wait()
            weight_copy(ups, up, up_sems, e, i, tile).wait()
            columns = slice(i * tile, (i + 1) * tile)
            x = rows_in[e]
            gate_value = jnp.dot(x, gate[e, :, columns], preferred_element_type=F32)
            up_value = jnp.dot(x, up[e, :, columns], preferred_element_type=F32)
            hidden[e, :, columns] = (jax.nn.silu(gate_value) * up_value).astype(BF16)
    for e in range(2):
        for i in range(down_tiles):
            weight_copy(downs, down, down_sems, e, i, down_tile).wait()
            columns = slice(i * down_tile, (i + 1) * down_tile)
            result = jnp.dot(hidden[e], down[e, :, columns], preferred_element_type=F32)
            result = result.astype(BF16)
            for k, out in enumerate(outs):
                out[e * capacity : (e + 1) * capacity, columns] = result[
                    k * capacity : (k + 1) * capacity
                ]


def run_hidden(chunks, gates, ups, downs, capacity, first):
    blocks = len(chunks[0])
    widths = tuple(chunk[0].shape[1] for chunk in chunks)
    _, width, units = gates[0].shape
    rows = blocks * capacity
    pieces = [part for chunk in chunks for part in chunk]
    tiles, down_tiles = 2, first // min(max(first, 1), 512)
    anywhere = pl.BlockSpec(memory_space=pl.ANY)
    vmem = pl.BlockSpec(memory_space=pltpu.VMEM)
    weights = [*gates, *ups] + (list(downs) if first else [])
    sent = blocks if first else 0
    scratch = [
        pltpu.VMEM((2, rows, width), BF16),
        pltpu.VMEM((2, width, units), BF16),
        pltpu.VMEM((2, width, units), BF16),
        pltpu.SemaphoreType.DMA((2, len(pieces))),
        pltpu.SemaphoreType.DMA((2, tiles)),
        pltpu.SemaphoreType.DMA((2, tiles)),
    ]
    if first:
        scratch += [
            pltpu.VMEM((2, units, first), BF16),
            pltpu.SemaphoreType.DMA((2, down_tiles)),
        ]
    return pl.pallas_call(
        functools.partial(experts_kernel, blocks, capacity, widths, first),
        out_shape=[jax.ShapeDtypeStruct((2 * capacity, first), BF16)] * sent
        + [jax.ShapeDtypeStruct((2, rows, units), BF16)],
        in_specs=[anywhere] * (len(pieces) + len(weights)),
        out_specs=[vmem] * (sent + 1),
        scratch_shapes=scratch,
        compiler_params=pltpu.CompilerParams(vmem_limit_bytes=46 * MIB),
        cost_estimate=pl.CostEstimate(
            flops=8 * rows * width * units + 4 * rows * first * units,
            bytes_accessed=8 * width * units + 4 * first * units + 8 * rows * width,
            transcendentals=2 * rows * units,
        ),
        name="experts",
    )(*pieces, *weights)


def down_kernel(blocks, capacity, start, tile, hidden, own, other, *refs):
    outs = refs[:blocks]
    down, sems = refs[blocks:]
    tiles = down.shape[2] // tile

    def copy(e, i):
        return pltpu.make_async_copy(
            (own, other)[e].at[0, :, pl.ds(start + i * tile, tile)],
            down.at[e, :, pl.ds(i * tile, tile)],
            sems.at[e, i],
        )

    for i in range(tiles):
        for e in range(2):
            copy(e, i).start()
    for i in range(tiles):
        for e in range(2):
            copy(e, i).wait()
            columns = slice(i * tile, (i + 1) * tile)
            result = jnp.dot(hidden[e], down[e, :, columns], preferred_element_type=F32)
            result = result.astype(BF16)
            for k, out in enumerate(outs):
                out[e * capacity : (e + 1) * capacity, columns] = result[
                    k * capacity : (k + 1) * capacity
                ]


def run_down(hidden, downs, start, width, blocks, capacity):
    _, rows, units = hidden.shape
    tile = min(width, 512)
    anywhere = pl.BlockSpec(memory_space=pl.ANY)
    vmem = pl.BlockSpec(memory_space=pltpu.VMEM)
    return pl.pallas_call(
        functools.partial(down_kernel, blocks, capacity, start, tile),
        out_shape=[jax.ShapeDtypeStruct((2 * capacity, width), BF16)] * blocks,
        in_specs=[vmem, anywhere, anywhere],
        out_specs=[vmem] * blocks,
        scratch_shapes=[
            pltpu.VMEM((2, units, width), BF16),
            pltpu.SemaphoreType.DMA((2, width // tile)),
        ],
        compiler_params=pltpu.CompilerParams(vmem_limit_bytes=20 * MIB),
        cost_estimate=pl.CostEstimate(
            flops=4 * rows * width * units,
            bytes_accessed=4 * width * units + 4 * rows * width + 4 * rows * units,
            transcendentals=0,
        ),
        name="down",
    )(hidden, *downs)


def run_near(rows, gates, ups, downs, capacity):
    width, blocks = rows[0].shape[1], len(rows)
    (hidden,) = run_hidden([rows], gates, ups, downs, capacity, 0)
    return run_down(hidden, downs, 0, width, blocks, capacity)


def run_far(chunks, gates, ups, downs, capacity):
    start, blocks = chunks[0][0].shape[1], len(chunks[0])
    *results, hidden = run_hidden(chunks, gates, ups, downs, capacity, start)
    results = [results]
    for chunk in chunks[1:]:
        width = chunk[0].shape[1]
        results.append(run_down(hidden, downs, start, width, blocks, capacity))
        start += width
    return results


def run_split(chunks, gates, ups, downs, capacity):
    blocks = len(chunks[0])
    rows = jnp.concatenate([jnp.stack(chunk) for chunk in chunks], axis=2)
    rows = rows.reshape(blocks, 2, capacity, -1)
    rows = lax.all_gather(rows, "tensor", axis=3, tiled=True)
    width = rows.shape[3]
    partial = []
    for e in range(2):
        x = rows[:, e].reshape(blocks * capacity, width)
        gate_value = jnp.dot(x, gates[e][0], preferred_element_type=F32)
        up_value = jnp.dot(x, ups[e][0], preferred_element_type=F32)
        hidden = (jax.nn.silu(gate_value) * up_value).astype(BF16)
        result = jnp.dot(hidden, downs[e][0], preferred_element_type=F32)
        partial.append(result.reshape(blocks, capacity, width))
    partial = jnp.stack(partial, axis=1).astype(BF16)
    reduced = lax.psum_scatter(partial, "tensor", scatter_dimension=3, tiled=True)
    reduced = reduced.reshape(blocks, 2 * capacity, -1)
    results, start = [], 0
    for chunk in chunks:
        stop = start + chunk[0].shape[1]
        results.append([reduced[k, :, start:stop] for k in range(blocks)])
        start = stop
    return results


def body(tokens, expert_ids, route_weights, gate_weight, up_weight, down_weight):
    groups = lax.axis_size("dp")
    count, _ = tokens.shape
    capacity = 4 * count // groups
    half = groups // 2
    blocks = half // 2
    me = lax.axis_index("dp").astype(jnp.int32).reshape(1)

    def swap(x, distance):
        return lax.ppermute(x, "dp", [(i, i ^ distance) for i in range(groups)])

    def spread(parts):
        order = sorted(range(1, blocks), key=lambda k: (-bin(k).count("1"), -k))
        moved = {k: swap(parts[k], 2 * k) for k in order}
        return [parts[0]] + [moved[k] for k in range(1, blocks)]

    whole = lax.axis_size("tensor") == 1

    ids, route = expert_ids.T, route_weights.T
    near_plan = make_plan(me, ids, route, blocks, capacity)
    picked = dispatch(near_plan, tokens, blocks, CHUNKS)
    far_tokens = []
    for i in range(CHUNKS):
        far_tokens.append(swap(picked[blocks + i], half))
    far_meta = swap(jnp.concatenate([ids.astype(F32), route], axis=0), half)
    near_rows = spread(picked[:blocks])
    gates = (gate_weight, swap(gate_weight, 1))
    ups = (up_weight, swap(up_weight, 1))
    downs = (down_weight, swap(down_weight, 1))
    far_plan = make_plan(me, far_meta[:2], far_meta[2:], blocks, capacity)
    far_rows = []
    for i in range(CHUNKS):
        far_parts = dispatch(far_plan, far_tokens[i], blocks)
        far_rows.append(spread(far_parts))
    if whole:
        near_results = run_near(near_rows, gates, ups, downs, capacity)
    else:
        near_results = run_split([near_rows], gates, ups, downs, capacity)[0]
    run = run_far if whole else run_split
    far_results = run(far_rows, gates, ups, downs, capacity)
    back = []
    for i in range(CHUNKS):
        returned = spread(far_results[i])
        mixed = mix(far_plan, returned, BF16)
        back.append(swap(mixed, half))
    returned = spread(near_results)
    near_sum = mix(near_plan, returned, F32)
    return (near_sum + jnp.concatenate(back, axis=1).astype(F32)).astype(BF16)


def solution(mesh):
    return jax.shard_map(
        body,
        mesh=mesh,
        in_specs=(
            P("dp", "tensor"),
            P("dp", None),
            P("dp", None),
            P("dp", None, "tensor"),
            P("dp", None, "tensor"),
            P("dp", "tensor", None),
        ),
        out_specs=P("dp", "tensor"),
        check_vma=False,
    )
```

profile of v0, /device:TPU:0, one launch (start us, length us, event | category | flops | bytes accessed | tf_op | source)
XLA Modules:
  0.0 208.4 jit_solution(10116305629876984548)
XLA Ops:
  2.4 3.6 %collective-permute-start.17 = (f32[4,256]{1,0:T(4,128)S(1)}, f32[4,256]{1,0:T(4,128)S(1)}, u32[]{:S(2)}, u32[]{:S(2)}) collective-permute-start(f32[4,256]{1,0:T(4,128)S(1)} %pad_maximum_fusion), channel_id=1, source_target_pairs={{0,16},{1,17},{2,18},{3,19},{4,20},{5,21},{6,22},{7,23},{8,24},{9,... | collective-permute-start | bytes 12296 | tf_op jit(solution)/shard_map/ppermute | solution.py:356
  11.6 6.7 %collective-permute-done.refs_1_ = bf16[64,2048]{1,0:T(8,128)(2,1)S(1)} collective-permute-done((bf16[64,2048]{1,0:T(8,128)(2,1)S(1)}, bf16[64,2048]{1,0:T(8,128)(2,1)S(1)}, u32[]{:S(2)}, u32[]{:S(2)}) %collective-permute-start) | collective-permute-done | bytes 262176 | tf_op jit(solution)/shard_map/ppermute | solution.py:356
  20.9 27.1 %collective-permute-done.18.tokens_ref = bf16[256,1024]{1,0:T(8,128)(2,1)S(1)} collective-permute-done((bf16[256,1024]{1,0:T(8,128)(2,1)S(1)}, bf16[256,1024]{1,0:T(8,128)(2,1)S(1)}, u32[]{:S(2)}, u32[]{:S(2)}) %collective-permute-start.18) | collective-permute-done | bytes 524320 | tf_op jit(solution)/shard_map/ppermute | solution.py:356
  50.3 4.5 %collective-permute-done.1.refs_2_ = bf16[64,2048]{1,0:T(8,128)(2,1)S(1)} collective-permute-done((bf16[64,2048]{1,0:T(8,128)(2,1)S(1)}, bf16[64,2048]{1,0:T(8,128)(2,1)S(1)}, u32[]{:S(2)}, u32[]{:S(2)}) %collective-permute-start.1) | collective-permute-done | bytes 262176 | tf_op jit(solution)/shard_map/ppermute | solution.py:356
  62.2 4.0 %collective-permute-done.20.refs_2_ = bf16[64,1024]{1,0:T(8,128)(2,1)S(1)} collective-permute-done((bf16[64,1024]{1,0:T(8,128)(2,1)S(1)}, bf16[64,1024]{1,0:T(8,128)(2,1)S(1)}, u32[]{:S(2)}, u32[]{:S(2)}) %collective-permute-start.20) | collective-permute-done | bytes 131104 | tf_op jit(solution)/shard_map/ppermute | solution.py:356
  66.2 2.9 %collective-permute-start.23 = (bf16[64,1024]{1,0:T(8,128)(2,1)S(1)}, bf16[64,1024]{1,0:T(8,128)(2,1)S(1)}, u32[]{:S(2)}, u32[]{:S(2)}) collective-permute-start(bf16[64,1024]{1,0:T(8,128)(2,1)S(1)} %get-tuple-element.90), channel_id=1, source_target_pairs={{0,10},{1,11},{2,8},{3,9},{4,14},{5,15},{6,12},{7,13},{8,2},{9,3},... | collective-permute-start | bytes 393224 | tf_op jit(solution)/shard_map/ppermute | solution.py:356
  78.9 3.3 %collective-permute-done.25.refs_7_ = bf16[64,1024]{1,0:T(8,128)(2,1)S(1)} collective-permute-done((bf16[64,1024]{1,0:T(8,128)(2,1)S(1)}, bf16[64,1024]{1,0:T(8,128)(2,1)S(1)}, u32[]{:S(2)}, u32[]{:S(2)}) %collective-permute-start.25) | collective-permute-done | bytes 131104 | tf_op jit(solution)/shard_map/ppermute | solution.py:356
  87.3 5.1 %collective-permute-done.29.refs_11_ = bf16[64,1024]{1,0:T(8,128)(2,1)S(1)} collective-permute-done((bf16[64,1024]{1,0:T(8,128)(2,1)S(1)}, bf16[64,1024]{1,0:T(8,128)(2,1)S(1)}, u32[]{:S(2)}, u32[]{:S(2)}) %collective-permute-start.29) | collective-permute-done | bytes 131104 | tf_op jit(solution)/shard_map/ppermute | solution.py:356
  94.6 4.1 %collective-permute-done.31.refs_13_ = bf16[64,1024]{1,0:T(8,128)(2,1)S(1)} collective-permute-done((bf16[64,1024]{1,0:T(8,128)(2,1)S(1)}, bf16[64,1024]{1,0:T(8,128)(2,1)S(1)}, u32[]{:S(2)}, u32[]{:S(2)}) %collective-permute-start.31) | collective-permute-done | bytes 131104 | tf_op jit(solution)/shard_map/ppermute | solution.py:356
  100.0 2.9 %collective-permute-start.2 = (bf16[64,2048]{1,0:T(8,128)(2,1)S(1)}, bf16[64,2048]{1,0:T(8,128)(2,1)S(1)}, u32[]{:S(2)}, u32[]{:S(2)}) collective-permute-start(bf16[64,2048]{1,0:T(8,128)(2,1)S(1)} %get-tuple-element.68), channel_id=1, source_target_pairs={{0,6},{1,7},{2,4},{3,5},{4,2},{5,3},{6,0},{7,1},{8,14},{9,15},{10,... | collective-permute-start | bytes 786440 | tf_op jit(solution)/shard_map/ppermute | solution.py:356
  102.9 4.4 %collective-permute-done.33.refs_15_ = bf16[64,1024]{1,0:T(8,128)(2,1)S(1)} collective-permute-done((bf16[64,1024]{1,0:T(8,128)(2,1)S(1)}, bf16[64,1024]{1,0:T(8,128)(2,1)S(1)}, u32[]{:S(2)}, u32[]{:S(2)}) %collective-permute-start.33) | collective-permute-done | bytes 131104 | tf_op jit(solution)/shard_map/ppermute | solution.py:356
  110.3 2.9 %collective-permute-start.6 = (bf16[64,2048]{1,0:T(8,128)(2,1)S(1)}, bf16[64,2048]{1,0:T(8,128)(2,1)S(1)}, u32[]{:S(2)}, u32[]{:S(2)}) collective-permute-start(bf16[64,2048]{1,0:T(8,128)(2,1)S(1)} %get-tuple-element.72), channel_id=1, source_target_pairs={{0,14},{1,15},{2,12},{3,13},{4,10},{5,11},{6,8},{7,9},{8,6},{9,7},... | collective-permute-start | bytes 786440 | tf_op jit(solution)/shard_map/ppermute | solution.py:356
  113.2 10.7 %experts.3 = (bf16[64,1024]{1,0:T(8,128)(2,1)S(1)}, bf16[64,1024]{1,0:T(8,128)(2,1)S(1)}, bf16[64,1024]{1,0:T(8,128)(2,1)S(1)}, bf16[64,1024]{1,0:T(8,128)(2,1)S...) custom-call(bf16[64,1024]{1,0:T(8,128)(2,1)S(1)} %get-tuple-element., ...), custom_call_target="tpu_custom_call" | custom-call | flops 5368709120 | bytes 25165824 | tf_op jit(solution)/shard_map/experts/pallas_call | solution.py:237
  124.5 2.9 %collective-permute-start.36 = (bf16[64,1024]{1,0:T(8,128)(2,1)S(1)}, bf16[64,1024]{1,0:T(8,128)(2,1)S(1)}, u32[]{:S(2)}, u32[]{:S(2)}) collective-permute-start(bf16[64,1024]{1,0:T(8,128)(2,1)S(1)} %get-tuple-element.105), channel_id=1, source_target_pairs={{0,6},{1,7},{2,4},{3,5},{4,2},{5,3},{6,0},{7,1},{8,14},{9,15},{10,... | collective-permute-start | bytes 393224 | tf_op jit(solution)/shard_map/ppermute | solution.py:356
  129.3 8.5 %experts.2.hidden = bf16[2,256,1024]{2,1,0:T(8,128)(2,1)S(1)} custom-call(bf16[64,2048]{1,0:T(8,128)(2,1)S(1)} %get-tuple-element.65.refs_0_, bf16[64,2048]{1,0:T(8,128)(2,1)S(1)} %collective-permute-done.refs_1_, bf16[64,2048]{1,0:T(8,128)(2,1)S(1)} %collective-permute-done.1.refs_2_, bf16[64,2048]{1,0:T(8,128)(2,1)S(1)} %collective-permute-done.2.refs_3_, ...), custom_call_target="tpu_custom_call" | custom-call | flops 4294967296 | bytes 20971520 | tf_op jit(solution)/shard_map/experts/pallas_call | solution.py:237
  137.8 2.8 %down.3 = (bf16[64,1024]{1,0:T(8,128)(2,1)S(1)}, bf16[64,1024]{1,0:T(8,128)(2,1)S(1)}, bf16[64,1024]{1,0:T(8,128)(2,1)S(1)}, bf16[64,1024]{1,0:T(8,128)(2,1)S(1)...) custom-call(bf16[2,256,1024]{2,1,0:T(8,128)(2,1)S(1)} %get-tuple-ele, ...), custom_call_target="tpu_custom_call" | custom-call | flops 1073741824 | bytes 6291456 | tf_op jit(solution)/shard_map/down/pallas_call | solution.py:286
  142.0 2.7 %collective-permute-start.40 = (bf16[64,1024]{1,0:T(8,128)(2,1)S(1)}, bf16[64,1024]{1,0:T(8,128)(2,1)S(1)}, u32[]{:S(2)}, u32[]{:S(2)}) collective-permute-start(bf16[64,1024]{1,0:T(8,128)(2,1)S(1)} %get-tuple-element.109), channel_id=1, source_target_pairs={{0,14},{1,15},{2,12},{3,13},{4,10},{5,11},{6,8},{7,9},{8,6},{9,7},... | collective-permute-start | bytes 393224 | tf_op jit(solution)/shard_map/ppermute | solution.py:356
  148.2 4.8 %down.2 = (bf16[64,2048]{1,0:T(8,128)(2,1)S(1)}, bf16[64,2048]{1,0:T(8,128)(2,1)S(1)}, bf16[64,2048]{1,0:T(8,128)(2,1)S(1)}, bf16[64,2048]{1,0:T(8,128)(2,1)S(1)...) custom-call(bf16[2,256,1024]{2,1,0:T(8,128)(2,1)S(1)} %experts.2.hid, ...), custom_call_target="tpu_custom_call" | custom-call | flops 2147483648 | bytes 11534336 | tf_op jit(solution)/shard_map/down/pallas_call | solution.py:286
  156.7 2.7 %collective-permute-done.43.refs_2_ = bf16[64,1024]{1,0:T(8,128)(2,1)S(1)} collective-permute-done((bf16[64,1024]{1,0:T(8,128)(2,1)S(1)}, bf16[64,1024]{1,0:T(8,128)(2,1)S(1)}, u32[]{:S(2)}, u32[]{:S(2)}) %collective-permute-start.43) | collective-permute-done | bytes 131104 | tf_op jit(solution)/shard_map/ppermute | solution.py:356
  165.2 3.7 %collective-permute-done.47.refs_6_ = bf16[64,1024]{1,0:T(8,128)(2,1)S(1)} collective-permute-done((bf16[64,1024]{1,0:T(8,128)(2,1)S(1)}, bf16[64,1024]{1,0:T(8,128)(2,1)S(1)}, u32[]{:S(2)}, u32[]{:S(2)}) %collective-permute-start.47) | collective-permute-done | bytes 131104 | tf_op jit(solution)/shard_map/ppermute | solution.py:356
  181.4 5.3 %collective-permute-done.13.refs_4_ = bf16[64,2048]{1,0:T(8,128)(2,1)S(1)} collective-permute-done((bf16[64,2048]{1,0:T(8,128)(2,1)S(1)}, bf16[64,2048]{1,0:T(8,128)(2,1)S(1)}, u32[]{:S(2)}, u32[]{:S(2)}) %collective-permute-start.13) | collective-permute-done | bytes 262176 | tf_op jit(solution)/shard_map/ppermute | solution.py:356
  186.8 10.7 %collective-permute-done.14.refs_5_ = bf16[64,2048]{1,0:T(8,128)(2,1)S(1)} collective-permute-done((bf16[64,2048]{1,0:T(8,128)(2,1)S(1)}, bf16[64,2048]{1,0:T(8,128)(2,1)S(1)}, u32[]{:S(2)}, u32[]{:S(2)}) %collective-permute-start.14) | collective-permute-done | bytes 262176 | tf_op jit(solution)/shard_map/ppermute | solution.py:356
  197.5 5.2 %collective-permute-done.15.refs_6_ = bf16[64,2048]{1,0:T(8,128)(2,1)S(1)} collective-permute-done((bf16[64,2048]{1,0:T(8,128)(2,1)S(1)}, bf16[64,2048]{1,0:T(8,128)(2,1)S(1)}, u32[]{:S(2)}, u32[]{:S(2)}) %collective-permute-start.15) | collective-permute-done | bytes 262176 | tf_op jit(solution)/shard_map/ppermute | solution.py:356
  202.7 2.9 %collective-permute-done.16.refs_7_ = bf16[64,2048]{1,0:T(8,128)(2,1)S(1)} collective-permute-done((bf16[64,2048]{1,0:T(8,128)(2,1)S(1)}, bf16[64,2048]{1,0:T(8,128)(2,1)S(1)}, u32[]{:S(2)}, u32[]{:S(2)}) %collective-permute-start.16) | collective-permute-done | bytes 262176 | tf_op jit(solution)/shard_map/ppermute | solution.py:356
  (102 shorter events, 73.6 us)
Async XLA Ops:
  0.0 107.3 %collective-permute-start.7 = (bf16[1,2048,1024]{2,1,0:T(8,128)(2,1)}, bf16[1,2048,1024]{2,1,0:T(8,128)(2,1)}, u32[]{:S(2)}, u32[]{:S(2)}) collective-permute-start(bf16[1,2048,1024]{2,1,0:T(8,128)(2,1)} %refs_16_.1), channel_id=1, source_target_pairs={{0,1},{1,0},{2,3},{3,2},{4,5},{5,4},{6,7},{7,6},{8,9},{9,8},{10,11... | collective-permute-start | bytes 12582920 | tf_op jit(solution)/shard_map/ppermute | solution.py:356
  0.5 107.8 %collective-permute-start.8 = (bf16[1,2048,1024]{2,1,0:T(8,128)(2,1)}, bf16[1,2048,1024]{2,1,0:T(8,128)(2,1)}, u32[]{:S(2)}, u32[]{:S(2)}) collective-permute-start(bf16[1,2048,1024]{2,1,0:T(8,128)(2,1)} %refs_18_.1), channel_id=1, source_target_pairs={{0,1},{1,0},{2,3},{3,2},{4,5},{5,4},{6,7},{7,6},{8,9},{9,8},{10,11... | collective-permute-start | bytes 12582920 | tf_op jit(solution)/shard_map/ppermute | solution.py:356
  0.5 109.7 %collective-permute-start.9 = (bf16[1,1024,2048]{2,1,0:T(8,128)(2,1)}, bf16[1,1024,2048]{2,1,0:T(8,128)(2,1)}, u32[]{:S(2)}, u32[]{:S(2)}) collective-permute-start(bf16[1,1024,2048]{2,1,0:T(8,128)(2,1)} %own.3), channel_id=1, source_target_pairs={{0,1},{1,0},{2,3},{3,2},{4,5},{5,4},{6,7},{7,6},{8,9},{9,8},{10,11... | collective-permute-start | bytes 12582920 | tf_op jit(solution)/shard_map/ppermute | solution.py:356
  9.7 38.2 %collective-permute-start.18 = (bf16[256,1024]{1,0:T(8,128)(2,1)S(1)}, bf16[256,1024]{1,0:T(8,128)(2,1)S(1)}, u32[]{:S(2)}, u32[]{:S(2)}) collective-permute-start(bf16[256,1024]{1,0:T(8,128)(2,1)S(1)} %get-tuple-element.84), channel_id=1, source_target_pairs={{0,16},{1,17},{2,18},{3,19},{4,20},{5,21},{6,22},{7,23},{8,24},{9,... | collective-permute-start | bytes 1572872 | tf_op jit(solution)/shard_map/ppermute | solution.py:356
  18.3 40.1 %collective-permute-start.26 = (bf16[256,1024]{1,0:T(8,128)(2,1)S(1)}, bf16[256,1024]{1,0:T(8,128)(2,1)S(1)}, u32[]{:S(2)}, u32[]{:S(2)}) collective-permute-start(bf16[256,1024]{1,0:T(8,128)(2,1)S(1)} %get-tuple-element.93), channel_id=1, source_target_pairs={{0,16},{1,17},{2,18},{3,19},{4,20},{5,21},{6,22},{7,23},{8,24},{9,... | collective-permute-start | bytes 1572872 | tf_op jit(solution)/shard_map/ppermute | solution.py:356
  100.0 23.9 %collective-permute-start.2 = (bf16[64,2048]{1,0:T(8,128)(2,1)S(1)}, bf16[64,2048]{1,0:T(8,128)(2,1)S(1)}, u32[]{:S(2)}, u32[]{:S(2)}) collective-permute-start(bf16[64,2048]{1,0:T(8,128)(2,1)S(1)} %get-tuple-element.68), channel_id=1, source_target_pairs={{0,6},{1,7},{2,4},{3,5},{4,2},{5,3},{6,0},{7,1},{8,14},{9,15},{10,... | collective-permute-start | bytes 786440 | tf_op jit(solution)/shard_map/ppermute | solution.py:356
  107.3 16.7 %collective-permute-start.3 = (bf16[64,2048]{1,0:T(8,128)(2,1)S(1)}, bf16[64,2048]{1,0:T(8,128)(2,1)S(1)}, u32[]{:S(2)}, u32[]{:S(2)}) collective-permute-start(bf16[64,2048]{1,0:T(8,128)(2,1)S(1)} %get-tuple-element.69), channel_id=1, source_target_pairs={{0,8},{1,9},{2,10},{3,11},{4,12},{5,13},{6,14},{7,15},{8,0},{9,1},... | collective-permute-start | bytes 786440 | tf_op jit(solution)/shard_map/ppermute | solution.py:356
  107.3 17.2 %collective-permute-start.4 = (bf16[64,2048]{1,0:T(8,128)(2,1)S(1)}, bf16[64,2048]{1,0:T(8,128)(2,1)S(1)}, u32[]{:S(2)}, u32[]{:S(2)}) collective-permute-start(bf16[64,2048]{1,0:T(8,128)(2,1)S(1)} %get-tuple-element.70), channel_id=1, source_target_pairs={{0,10},{1,11},{2,8},{3,9},{4,14},{5,15},{6,12},{7,13},{8,2},{9,3},... | collective-permute-start | bytes 786440 | tf_op jit(solution)/shard_map/ppermute | solution.py:356
  108.2 19.2 %collective-permute-start.5 = (bf16[64,2048]{1,0:T(8,128)(2,1)S(1)}, bf16[64,2048]{1,0:T(8,128)(2,1)S(1)}, u32[]{:S(2)}, u32[]{:S(2)}) collective-permute-start(bf16[64,2048]{1,0:T(8,128)(2,1)S(1)} %get-tuple-element.71), channel_id=1, source_target_pairs={{0,12},{1,13},{2,14},{3,15},{4,8},{5,9},{6,10},{7,11},{8,4},{9,5},... | collective-permute-start | bytes 786440 | tf_op jit(solution)/shard_map/ppermute | solution.py:356
  110.3 17.4 %collective-permute-start.6 = (bf16[64,2048]{1,0:T(8,128)(2,1)S(1)}, bf16[64,2048]{1,0:T(8,128)(2,1)S(1)}, u32[]{:S(2)}, u32[]{:S(2)}) collective-permute-start(bf16[64,2048]{1,0:T(8,128)(2,1)S(1)} %get-tuple-element.72), channel_id=1, source_target_pairs={{0,14},{1,15},{2,12},{3,13},{4,10},{5,11},{6,8},{7,9},{8,6},{9,7},... | collective-permute-start | bytes 786440 | tf_op jit(solution)/shard_map/ppermute | solution.py:356
  123.9 16.7 %collective-permute-start.34 = (bf16[64,1024]{1,0:T(8,128)(2,1)S(1)}, bf16[64,1024]{1,0:T(8,128)(2,1)S(1)}, u32[]{:S(2)}, u32[]{:S(2)}) collective-permute-start(bf16[64,1024]{1,0:T(8,128)(2,1)S(1)} %get-tuple-element.103), channel_id=1, source_target_pairs={{0,2},{1,3},{2,0},{3,1},{4,6},{5,7},{6,4},{7,5},{8,10},{9,11},{10,... | collective-permute-start | bytes 393224 | tf_op jit(solution)/shard_map/ppermute | solution.py:356
  124.0 18.0 %collective-permute-start.35 = (bf16[64,1024]{1,0:T(8,128)(2,1)S(1)}, bf16[64,1024]{1,0:T(8,128)(2,1)S(1)}, u32[]{:S(2)}, u32[]{:S(2)}) collective-permute-start(bf16[64,1024]{1,0:T(8,128)(2,1)S(1)} %get-tuple-element.104), channel_id=1, source_target_pairs={{0,4},{1,5},{2,6},{3,7},{4,0},{5,1},{6,2},{7,3},{8,12},{9,13},{10,... | collective-permute-start | bytes 393224 | tf_op jit(solution)/shard_map/ppermute | solution.py:356
  124.5 20.2 %collective-permute-start.36 = (bf16[64,1024]{1,0:T(8,128)(2,1)S(1)}, bf16[64,1024]{1,0:T(8,128)(2,1)S(1)}, u32[]{:S(2)}, u32[]{:S(2)}) collective-permute-start(bf16[64,1024]{1,0:T(8,128)(2,1)S(1)} %get-tuple-element.105), channel_id=1, source_target_pairs={{0,6},{1,7},{2,4},{3,5},{4,2},{5,3},{6,0},{7,1},{8,14},{9,15},{10,... | collective-permute-start | bytes 393224 | tf_op jit(solution)/shard_map/ppermute | solution.py:356
  127.5 17.6 %collective-permute-start.37 = (bf16[64,1024]{1,0:T(8,128)(2,1)S(1)}, bf16[64,1024]{1,0:T(8,128)(2,1)S(1)}, u32[]{:S(2)}, u32[]{:S(2)}) collective-permute-start(bf16[64,1024]{1,0:T(8,128)(2,1)S(1)} %get-tuple-element.106), channel_id=1, source_target_pairs={{0,8},{1,9},{2,10},{3,11},{4,12},{5,13},{6,14},{7,15},{8,0},{9,1},... | collective-permute-start | bytes 393224 | tf_op jit(solution)/shard_map/ppermute | solution.py:356
  127.6 17.9 %collective-permute-start.38 = (bf16[64,1024]{1,0:T(8,128)(2,1)S(1)}, bf16[64,1024]{1,0:T(8,128)(2,1)S(1)}, u32[]{:S(2)}, u32[]{:S(2)}) collective-permute-start(bf16[64,1024]{1,0:T(8,128)(2,1)S(1)} %get-tuple-element.107), channel_id=1, source_target_pairs={{0,10},{1,11},{2,8},{3,9},{4,14},{5,15},{6,12},{7,13},{8,2},{9,3},... | collective-permute-start | bytes 393224 | tf_op jit(solution)/shard_map/ppermute | solution.py:356
  153.1 24.3 %collective-permute-start.10 = (bf16[64,2048]{1,0:T(8,128)(2,1)S(1)}, bf16[64,2048]{1,0:T(8,128)(2,1)S(1)}, u32[]{:S(2)}, u32[]{:S(2)}) collective-permute-start(bf16[64,2048]{1,0:T(8,128)(2,1)S(1)} %get-tuple-element.74), channel_id=1, source_target_pairs={{0,2},{1,3},{2,0},{3,1},{4,6},{5,7},{6,4},{7,5},{8,10},{9,11},{10,... | collective-permute-start | bytes 786440 | tf_op jit(solution)/shard_map/ppermute | solution.py:356
  162.4 16.2 %collective-permute-start.11 = (bf16[64,2048]{1,0:T(8,128)(2,1)S(1)}, bf16[64,2048]{1,0:T(8,128)(2,1)S(1)}, u32[]{:S(2)}, u32[]{:S(2)}) collective-permute-start(bf16[64,2048]{1,0:T(8,128)(2,1)S(1)} %get-tuple-element.75), channel_id=1, source_target_pairs={{0,4},{1,5},{2,6},{3,7},{4,0},{5,1},{6,2},{7,3},{8,12},{9,13},{10,... | collective-permute-start | bytes 786440 | tf_op jit(solution)/shard_map/ppermute | solution.py:356
  163.5 15.8 %collective-permute-start.12 = (bf16[64,2048]{1,0:T(8,128)(2,1)S(1)}, bf16[64,2048]{1,0:T(8,128)(2,1)S(1)}, u32[]{:S(2)}, u32[]{:S(2)}) collective-permute-start(bf16[64,2048]{1,0:T(8,128)(2,1)S(1)} %get-tuple-element.76), channel_id=1, source_target_pairs={{0,6},{1,7},{2,4},{3,5},{4,2},{5,3},{6,0},{7,1},{8,14},{9,15},{10,... | collective-permute-start | bytes 786440 | tf_op jit(solution)/shard_map/ppermute | solution.py:356
  169.0 17.8 %collective-permute-start.13 = (bf16[64,2048]{1,0:T(8,128)(2,1)S(1)}, bf16[64,2048]{1,0:T(8,128)(2,1)S(1)}, u32[]{:S(2)}, u32[]{:S(2)}) collective-permute-start(bf16[64,2048]{1,0:T(8,128)(2,1)S(1)} %get-tuple-element.77), channel_id=1, source_target_pairs={{0,8},{1,9},{2,10},{3,11},{4,12},{5,13},{6,14},{7,15},{8,0},{9,1},... | collective-permute-start | bytes 786440 | tf_op jit(solution)/shard_map/ppermute | solution.py:356
  173.4 33.6 %collective-permute-start.41 = (bf16[256,1024]{1,0:T(8,128)(2,1)S(1)}, bf16[256,1024]{1,0:T(8,128)(2,1)S(1)}, u32[]{:S(2)}, u32[]{:S(2)}) collective-permute-start(bf16[256,1024]{1,0:T(8,128)(2,1)S(1)} %mix.4), channel_id=1, source_target_pairs={{0,16},{1,17},{2,18},{3,19},{4,20},{5,21},{6,22},{7,23},{8,24},{9,... | collective-permute-start | bytes 1572872 | tf_op jit(solution)/shard_map/ppermute | solution.py:356
  177.4 29.7 %collective-permute-start.49 = (bf16[256,1024]{1,0:T(8,128)(2,1)S(1)}, bf16[256,1024]{1,0:T(8,128)(2,1)S(1)}, u32[]{:S(2)}, u32[]{:S(2)}) collective-permute-start(bf16[256,1024]{1,0:T(8,128)(2,1)S(1)} %mix.5), channel_id=1, source_target_pairs={{0,16},{1,17},{2,18},{3,19},{4,20},{5,21},{6,22},{7,23},{8,24},{9,... | collective-permute-start | bytes 1572872 | tf_op jit(solution)/shard_map/ppermute | solution.py:356
  178.5 19.0 %collective-permute-start.14 = (bf16[64,2048]{1,0:T(8,128)(2,1)S(1)}, bf16[64,2048]{1,0:T(8,128)(2,1)S(1)}, u32[]{:S(2)}, u32[]{:S(2)}) collective-permute-start(bf16[64,2048]{1,0:T(8,128)(2,1)S(1)} %get-tuple-element.78), channel_id=1, source_target_pairs={{0,10},{1,11},{2,8},{3,9},{4,14},{5,15},{6,12},{7,13},{8,2},{9,3},... | collective-permute-start | bytes 786440 | tf_op jit(solution)/shard_map/ppermute | solution.py:356
  179.3 23.4 %collective-permute-start.15 = (bf16[64,2048]{1,0:T(8,128)(2,1)S(1)}, bf16[64,2048]{1,0:T(8,128)(2,1)S(1)}, u32[]{:S(2)}, u32[]{:S(2)}) collective-permute-start(bf16[64,2048]{1,0:T(8,128)(2,1)S(1)} %get-tuple-element.79), channel_id=1, source_target_pairs={{0,12},{1,13},{2,14},{3,15},{4,8},{5,9},{6,10},{7,11},{8,4},{9,5},... | collective-permute-start | bytes 786440 | tf_op jit(solution)/shard_map/ppermute | solution.py:356
  186.8 18.8 %collective-permute-start.16 = (bf16[64,2048]{1,0:T(8,128)(2,1)S(1)}, bf16[64,2048]{1,0:T(8,128)(2,1)S(1)}, u32[]{:S(2)}, u32[]{:S(2)}) collective-permute-start(bf16[64,2048]{1,0:T(8,128)(2,1)S(1)} %get-tuple-element.80), channel_id=1, source_target_pairs={{0,14},{1,15},{2,12},{3,13},{4,10},{5,11},{6,8},{7,9},{8,6},{9,7},... | collective-permute-start | bytes 786440 | tf_op jit(solution)/shard_map/ppermute | solution.py:356
  (31 other events, 247.4 us)
where the time goes:
time: 209 us; the launch traced here: 208 us
  waiting for transfers between devices  102 us (49%)
  starting transfers between devices  65.4 us (31%)
  Pallas kernels  35 us (17%)
  other arithmetic  2.68 us (1%)
  local copies, waits for them, and re-layouts  2.59 us (1%)
    ppermute x50, waiting for transfers between devices, swap(): return lax.ppermute(x, 'dp', [(i, i ^ distance) for i in range(groups)])  102 us
    ppermute x50, starting transfers between devices, swap(): return lax.ppermute(x, 'dp', [(i, i ^ distance) for i in range(groups)])  65.4 us
    pallas_call x2, Pallas kernels, run_hidden(): pl.pallas_call(functools.partial(experts_kernel, blocks, capacity, widths...  19.2 us
    pallas_call x2, Pallas kernels, run_down(): pl.pallas_call(functools.partial(down_kernel, blocks, capacity, start, ti...  7.62 us
    pallas_call x3, Pallas kernels, mix(): pl.pallas_call(functools.partial(mix_kernel, blocks), out_shape=jax.Shape...  5.71 us
  transfers between devices with their start and end apart: 50, of which 23 were waited for; matrix products, arithmetic and copies ran while one was open for 1% of the time, Pallas kernels for 17%

commit v1 on v0

--- a/solution.py
+++ b/solution.py
@@ -292,7 +292,7 @@
             pltpu.VMEM((2, units, width), BF16),
             pltpu.SemaphoreType.DMA((2, width // tile)),
         ],
-        compiler_params=pltpu.CompilerParams(vmem_limit_bytes=20 * MIB),
+        compiler_params=pltpu.CompilerParams(vmem_limit_bytes=46 * MIB),
         cost_estimate=pl.CostEstimate(
             flops=4 * rows * width * units,
             bytes_accessed=4 * width * units + 4 * rows * width + 4 * rows * units,
@@ -357,7 +357,9 @@
 
     def spread(parts):
         order = sorted(range(1, blocks), key=lambda k: (-bin(k).count("1"), -k))
-        moved = {k: swap(parts[k], 2 * k) for k in order}
+        moved = {}
+        for k in order:
+            moved[k] = swap(parts[k], 2 * k)
         return [parts[0]] + [moved[k] for k in range(1, blocks)]
 
     whole = lax.axis_size("tensor") == 1
@@ -370,9 +372,13 @@
         far_tokens.append(swap(picked[blocks + i], half))
     far_meta = swap(jnp.concatenate([ids.astype(F32), route], axis=0), half)
     near_rows = spread(picked[:blocks])
-    gates = (gate_weight, swap(gate_weight, 1))
-    ups = (up_weight, swap(up_weight, 1))
-    downs = (down_weight, swap(down_weight, 1))
+    stay = [
+        pltpu.with_memory_space_constraint(w, pltpu.HBM) if whole else w
+        for w in (gate_weight, up_weight, down_weight)
+    ]
+    gates = (stay[0], swap(gate_weight, 1))
+    ups = (stay[1], swap(up_weight, 1))
+    downs = (stay[2], swap(down_weight, 1))
     far_plan = make_plan(me, far_meta[:2], far_meta[2:], blocks, capacity)
     far_rows = []
     for i in range(CHUNKS):

time: 209 us -> 209 us (level)
  no operation moved by 1% of the time
where the time goes in v1:
time: 209 us
  waiting for transfers between devices  103 us (49%)
  starting transfers between devices  64.6 us (31%)
  Pallas kernels  35.5 us (17%)
  other arithmetic  2.68 us (1%)
  local copies, waits for them, and re-layouts  2.59 us (1%)
    ppermute x50, waiting for transfers between devices, swap(): return lax.ppermute(x, 'dp', [(i, i ^ distance) for i in range(groups)])  103 us
    ppermute x50, starting transfers between devices, swap(): return lax.ppermute(x, 'dp', [(i, i ^ distance) for i in range(groups)])  64.6 us
    pallas_call x2, Pallas kernels, run_hidden(): pl.pallas_call(functools.partial(experts_kernel, blocks, capacity, widths...  19.5 us
    pallas_call x2, Pallas kernels, run_down(): pl.pallas_call(functools.partial(down_kernel, blocks, capacity, start, ti...  7.85 us
    pallas_call x3, Pallas kernels, mix(): pl.pallas_call(functools.partial(mix_kernel, blocks), out_shape=jax.Shape...  5.71 us
  transfers between devices with their start and end apart: 50, of which 23 were waited for; matrix products, arithmetic and copies ran while one was open for 1% of the time, Pallas kernels for 17%

profile of v1, /device:TPU:0, one launch (start us, length us, event | category | flops | bytes accessed | tf_op | source)
XLA Modules:
  0.0 208.6 jit_solution(4476505501602408830)
XLA Ops:
  2.4 3.6 %collective-permute-start.17 = (f32[4,256]{1,0:T(4,128)S(1)}, f32[4,256]{1,0:T(4,128)S(1)}, u32[]{:S(2)}, u32[]{:S(2)}) collective-permute-start(f32[4,256]{1,0:T(4,128)S(1)} %pad_maximum_fusion), channel_id=1, source_target_pairs={{0,16},{1,17},{2,18},{3,19},{4,20},{5,21},{6,22},{7,23},{8,24},{9,... | collective-permute-start | bytes 12296 | tf_op jit(solution)/shard_map/ppermute | solution.py:356
  11.6 6.7 %collective-permute-done.refs_1_ = bf16[64,2048]{1,0:T(8,128)(2,1)S(1)} collective-permute-done((bf16[64,2048]{1,0:T(8,128)(2,1)S(1)}, bf16[64,2048]{1,0:T(8,128)(2,1)S(1)}, u32[]{:S(2)}, u32[]{:S(2)}) %collective-permute-start) | collective-permute-done | bytes 262176 | tf_op jit(solution)/shard_map/ppermute | solution.py:356
  20.9 27.1 %collective-permute-done.18.tokens_ref = bf16[256,1024]{1,0:T(8,128)(2,1)S(1)} collective-permute-done((bf16[256,1024]{1,0:T(8,128)(2,1)S(1)}, bf16[256,1024]{1,0:T(8,128)(2,1)S(1)}, u32[]{:S(2)}, u32[]{:S(2)}) %collective-permute-start.18) | collective-permute-done | bytes 524320 | tf_op jit(solution)/shard_map/ppermute | solution.py:356
  50.3 4.5 %collective-permute-done.1.refs_2_ = bf16[64,2048]{1,0:T(8,128)(2,1)S(1)} collective-permute-done((bf16[64,2048]{1,0:T(8,128)(2,1)S(1)}, bf16[64,2048]{1,0:T(8,128)(2,1)S(1)}, u32[]{:S(2)}, u32[]{:S(2)}) %collective-permute-start.1) | collective-permute-done | bytes 262176 | tf_op jit(solution)/shard_map/ppermute | solution.py:356
  62.2 4.0 %collective-permute-done.20.refs_2_ = bf16[64,1024]{1,0:T(8,128)(2,1)S(1)} collective-permute-done((bf16[64,1024]{1,0:T(8,128)(2,1)S(1)}, bf16[64,1024]{1,0:T(8,128)(2,1)S(1)}, u32[]{:S(2)}, u32[]{:S(2)}) %collective-permute-start.20) | collective-permute-done | bytes 131104 | tf_op jit(solution)/shard_map/ppermute | solution.py:356
  66.2 2.9 %collective-permute-start.23 = (bf16[64,1024]{1,0:T(8,128)(2,1)S(1)}, bf16[64,1024]{1,0:T(8,128)(2,1)S(1)}, u32[]{:S(2)}, u32[]{:S(2)}) collective-permute-start(bf16[64,1024]{1,0:T(8,128)(2,1)S(1)} %get-tuple-element.90), channel_id=1, source_target_pairs={{0,10},{1,11},{2,8},{3,9},{4,14},{5,15},{6,12},{7,13},{8,2},{9,3},... | collective-permute-start | bytes 393224 | tf_op jit(solution)/shard_map/ppermute | solution.py:356
  78.9 3.3 %collective-permute-done.25.refs_7_ = bf16[64,1024]{1,0:T(8,128)(2,1)S(1)} collective-permute-done((bf16[64,1024]{1,0:T(8,128)(2,1)S(1)}, bf16[64,1024]{1,0:T(8,128)(2,1)S(1)}, u32[]{:S(2)}, u32[]{:S(2)}) %collective-permute-start.25) | collective-permute-done | bytes 131104 | tf_op jit(solution)/shard_map/ppermute | solution.py:356
  87.3 5.1 %collective-permute-done.29.refs_11_ = bf16[64,1024]{1,0:T(8,128)(2,1)S(1)} collective-permute-done((bf16[64,1024]{1,0:T(8,128)(2,1)S(1)}, bf16[64,1024]{1,0:T(8,128)(2,1)S(1)}, u32[]{:S(2)}, u32[]{:S(2)}) %collective-permute-start.29) | collective-permute-done | bytes 131104 | tf_op jit(solution)/shard_map/ppermute | solution.py:356
  94.6 4.1 %collective-permute-done.31.refs_13_ = bf16[64,1024]{1,0:T(8,128)(2,1)S(1)} collective-permute-done((bf16[64,1024]{1,0:T(8,128)(2,1)S(1)}, bf16[64,1024]{1,0:T(8,128)(2,1)S(1)}, u32[]{:S(2)}, u32[]{:S(2)}) %collective-permute-start.31) | collective-permute-done | bytes 131104 | tf_op jit(solution)/shard_map/ppermute | solution.py:356
  100.0 2.9 %collective-permute-start.2 = (bf16[64,2048]{1,0:T(8,128)(2,1)S(1)}, bf16[64,2048]{1,0:T(8,128)(2,1)S(1)}, u32[]{:S(2)}, u32[]{:S(2)}) collective-permute-start(bf16[64,2048]{1,0:T(8,128)(2,1)S(1)} %get-tuple-element.68), channel_id=1, source_target_pairs={{0,6},{1,7},{2,4},{3,5},{4,2},{5,3},{6,0},{7,1},{8,14},{9,15},{10,... | collective-permute-start | bytes 786440 | tf_op jit(solution)/shard_map/ppermute | solution.py:356
  102.9 4.4 %collective-permute-done.33.refs_15_ = bf16[64,1024]{1,0:T(8,128)(2,1)S(1)} collective-permute-done((bf16[64,1024]{1,0:T(8,128)(2,1)S(1)}, bf16[64,1024]{1,0:T(8,128)(2,1)S(1)}, u32[]{:S(2)}, u32[]{:S(2)}) %collective-permute-start.33) | collective-permute-done | bytes 131104 | tf_op jit(solution)/shard_map/ppermute | solution.py:356
  110.3 2.9 %collective-permute-start.6 = (bf16[64,2048]{1,0:T(8,128)(2,1)S(1)}, bf16[64,2048]{1,0:T(8,128)(2,1)S(1)}, u32[]{:S(2)}, u32[]{:S(2)}) collective-permute-start(bf16[64,2048]{1,0:T(8,128)(2,1)S(1)} %get-tuple-element.72), channel_id=1, source_target_pairs={{0,14},{1,15},{2,12},{3,13},{4,10},{5,11},{6,8},{7,9},{8,6},{9,7},... | collective-permute-start | bytes 786440 | tf_op jit(solution)/shard_map/ppermute | solution.py:356
  113.2 10.6 %experts.3 = (bf16[64,1024]{1,0:T(8,128)(2,1)S(1)}, bf16[64,1024]{1,0:T(8,128)(2,1)S(1)}, bf16[64,1024]{1,0:T(8,128)(2,1)S(1)}, bf16[64,1024]{1,0:T(8,128)(2,1)S...) custom-call(bf16[64,1024]{1,0:T(8,128)(2,1)S(1)} %get-tuple-element., ...), custom_call_target="tpu_custom_call" | custom-call | flops 5368709120 | bytes 25165824 | tf_op jit(solution)/shard_map/experts/pallas_call | solution.py:237
  124.4 2.9 %collective-permute-start.36 = (bf16[64,1024]{1,0:T(8,128)(2,1)S(1)}, bf16[64,1024]{1,0:T(8,128)(2,1)S(1)}, u32[]{:S(2)}, u32[]{:S(2)}) collective-permute-start(bf16[64,1024]{1,0:T(8,128)(2,1)S(1)} %get-tuple-element.105), channel_id=1, source_target_pairs={{0,6},{1,7},{2,4},{3,5},{4,2},{5,3},{6,0},{7,1},{8,14},{9,15},{10,... | collective-permute-start | bytes 393224 | tf_op jit(solution)/shard_map/ppermute | solution.py:356
  129.3 8.9 %experts.2.hidden = bf16[2,256,1024]{2,1,0:T(8,128)(2,1)S(1)} custom-call(bf16[64,2048]{1,0:T(8,128)(2,1)S(1)} %get-tuple-element.65.refs_0_, bf16[64,2048]{1,0:T(8,128)(2,1)S(1)} %collective-permute-done.refs_1_, bf16[64,2048]{1,0:T(8,128)(2,1)S(1)} %collective-permute-done.1.refs_2_, bf16[64,2048]{1,0:T(8,128)(2,1)S(1)} %collective-permute-done.2.refs_3_, ...), custom_call_target="tpu_custom_call" | custom-call | flops 4294967296 | bytes 20971520 | tf_op jit(solution)/shard_map/experts/pallas_call | solution.py:237
  138.2 3.0 %down.3 = (bf16[64,1024]{1,0:T(8,128)(2,1)S(1)}, bf16[64,1024]{1,0:T(8,128)(2,1)S(1)}, bf16[64,1024]{1,0:T(8,128)(2,1)S(1)}, bf16[64,1024]{1,0:T(8,128)(2,1)S(1)...) custom-call(bf16[2,256,1024]{2,1,0:T(8,128)(2,1)S(1)} %get-tuple-ele, ...), custom_call_target="tpu_custom_call" | custom-call | flops 1073741824 | bytes 6291456 | tf_op jit(solution)/shard_map/down/pallas_call | solution.py:286
  148.7 4.8 %down.2 = (bf16[64,2048]{1,0:T(8,128)(2,1)S(1)}, bf16[64,2048]{1,0:T(8,128)(2,1)S(1)}, bf16[64,2048]{1,0:T(8,128)(2,1)S(1)}, bf16[64,2048]{1,0:T(8,128)(2,1)S(1)...) custom-call(bf16[2,256,1024]{2,1,0:T(8,128)(2,1)S(1)} %experts.2.hid, ...), custom_call_target="tpu_custom_call" | custom-call | flops 2147483648 | bytes 11534336 | tf_op jit(solution)/shard_map/down/pallas_call | solution.py:286
  157.1 2.9 %collective-permute-done.43.refs_2_ = bf16[64,1024]{1,0:T(8,128)(2,1)S(1)} collective-permute-done((bf16[64,1024]{1,0:T(8,128)(2,1)S(1)}, bf16[64,1024]{1,0:T(8,128)(2,1)S(1)}, u32[]{:S(2)}, u32[]{:S(2)}) %collective-permute-start.43) | collective-permute-done | bytes 131104 | tf_op jit(solution)/shard_map/ppermute | solution.py:356
  165.9 3.2 %collective-permute-done.47.refs_6_ = bf16[64,1024]{1,0:T(8,128)(2,1)S(1)} collective-permute-done((bf16[64,1024]{1,0:T(8,128)(2,1)S(1)}, bf16[64,1024]{1,0:T(8,128)(2,1)S(1)}, u32[]{:S(2)}, u32[]{:S(2)}) %collective-permute-start.47) | collective-permute-done | bytes 131104 | tf_op jit(solution)/shard_map/ppermute | solution.py:356
  171.2 2.9 %collective-permute-done.48.refs_7_ = bf16[64,1024]{1,0:T(8,128)(2,1)S(1)} collective-permute-done((bf16[64,1024]{1,0:T(8,128)(2,1)S(1)}, bf16[64,1024]{1,0:T(8,128)(2,1)S(1)}, u32[]{:S(2)}, u32[]{:S(2)}) %collective-permute-start.48) | collective-permute-done | bytes 131104 | tf_op jit(solution)/shard_map/ppermute | solution.py:356
  182.1 4.9 %collective-permute-done.13.refs_4_ = bf16[64,2048]{1,0:T(8,128)(2,1)S(1)} collective-permute-done((bf16[64,2048]{1,0:T(8,128)(2,1)S(1)}, bf16[64,2048]{1,0:T(8,128)(2,1)S(1)}, u32[]{:S(2)}, u32[]{:S(2)}) %collective-permute-start.13) | collective-permute-done | bytes 262176 | tf_op jit(solution)/shard_map/ppermute | solution.py:356
  187.0 11.1 %collective-permute-done.14.refs_5_ = bf16[64,2048]{1,0:T(8,128)(2,1)S(1)} collective-permute-done((bf16[64,2048]{1,0:T(8,128)(2,1)S(1)}, bf16[64,2048]{1,0:T(8,128)(2,1)S(1)}, u32[]{:S(2)}, u32[]{:S(2)}) %collective-permute-start.14) | collective-permute-done | bytes 262176 | tf_op jit(solution)/shard_map/ppermute | solution.py:356
  198.1 4.8 %collective-permute-done.15.refs_6_ = bf16[64,2048]{1,0:T(8,128)(2,1)S(1)} collective-permute-done((bf16[64,2048]{1,0:T(8,128)(2,1)S(1)}, bf16[64,2048]{1,0:T(8,128)(2,1)S(1)}, u32[]{:S(2)}, u32[]{:S(2)}) %collective-permute-start.15) | collective-permute-done | bytes 262176 | tf_op jit(solution)/shard_map/ppermute | solution.py:356
  202.9 2.9 %collective-permute-done.16.refs_7_ = bf16[64,2048]{1,0:T(8,128)(2,1)S(1)} collective-permute-done((bf16[64,2048]{1,0:T(8,128)(2,1)S(1)}, bf16[64,2048]{1,0:T(8,128)(2,1)S(1)}, u32[]{:S(2)}, u32[]{:S(2)}) %collective-permute-start.16) | collective-permute-done | bytes 262176 | tf_op jit(solution)/shard_map/ppermute | solution.py:356
  (98 shorter events, 73.9 us)
Async XLA Ops:
  0.0 107.3 %collective-permute-start.7 = (bf16[1,2048,1024]{2,1,0:T(8,128)(2,1)}, bf16[1,2048,1024]{2,1,0:T(8,128)(2,1)}, u32[]{:S(2)}, u32[]{:S(2)}) collective-permute-start(bf16[1,2048,1024]{2,1,0:T(8,128)(2,1)} %refs_16_.1), channel_id=1, source_target_pairs={{0,1},{1,0},{2,3},{3,2},{4,5},{5,4},{6,7},{7,6},{8,9},{9,8},{10,11... | collective-permute-start | bytes 12582920 | tf_op jit(solution)/shard_map/ppermute | solution.py:356
  0.5 107.8 %collective-permute-start.8 = (bf16[1,2048,1024]{2,1,0:T(8,128)(2,1)}, bf16[1,2048,1024]{2,1,0:T(8,128)(2,1)}, u32[]{:S(2)}, u32[]{:S(2)}) collective-permute-start(bf16[1,2048,1024]{2,1,0:T(8,128)(2,1)} %refs_18_.1), channel_id=1, source_target_pairs={{0,1},{1,0},{2,3},{3,2},{4,5},{5,4},{6,7},{7,6},{8,9},{9,8},{10,11... | collective-permute-start | bytes 12582920 | tf_op jit(solution)/shard_map/ppermute | solution.py:356
  0.5 109.7 %collective-permute-start.9 = (bf16[1,1024,2048]{2,1,0:T(8,128)(2,1)}, bf16[1,1024,2048]{2,1,0:T(8,128)(2,1)}, u32[]{:S(2)}, u32[]{:S(2)}) collective-permute-start(bf16[1,1024,2048]{2,1,0:T(8,128)(2,1)} %own.3), channel_id=1, source_target_pairs={{0,1},{1,0},{2,3},{3,2},{4,5},{5,4},{6,7},{7,6},{8,9},{9,8},{10,11... | collective-permute-start | bytes 12582920 | tf_op jit(solution)/shard_map/ppermute | solution.py:356
  9.7 38.2 %collective-permute-start.18 = (bf16[256,1024]{1,0:T(8,128)(2,1)S(1)}, bf16[256,1024]{1,0:T(8,128)(2,1)S(1)}, u32[]{:S(2)}, u32[]{:S(2)}) collective-permute-start(bf16[256,1024]{1,0:T(8,128)(2,1)S(1)} %get-tuple-element.84), channel_id=1, source_target_pairs={{0,16},{1,17},{2,18},{3,19},{4,20},{5,21},{6,22},{7,23},{8,24},{9,... | collective-permute-start | bytes 1572872 | tf_op jit(solution)/shard_map/ppermute | solution.py:356
  18.3 40.1 %collective-permute-start.26 = (bf16[256,1024]{1,0:T(8,128)(2,1)S(1)}, bf16[256,1024]{1,0:T(8,128)(2,1)S(1)}, u32[]{:S(2)}, u32[]{:S(2)}) collective-permute-start(bf16[256,1024]{1,0:T(8,128)(2,1)S(1)} %get-tuple-element.93), channel_id=1, source_target_pairs={{0,16},{1,17},{2,18},{3,19},{4,20},{5,21},{6,22},{7,23},{8,24},{9,... | collective-permute-start | bytes 1572872 | tf_op jit(solution)/shard_map/ppermute | solution.py:356
  100.0 23.8 %collective-permute-start.2 = (bf16[64,2048]{1,0:T(8,128)(2,1)S(1)}, bf16[64,2048]{1,0:T(8,128)(2,1)S(1)}, u32[]{:S(2)}, u32[]{:S(2)}) collective-permute-start(bf16[64,2048]{1,0:T(8,128)(2,1)S(1)} %get-tuple-element.68), channel_id=1, source_target_pairs={{0,6},{1,7},{2,4},{3,5},{4,2},{5,3},{6,0},{7,1},{8,14},{9,15},{10,... | collective-permute-start | bytes 786440 | tf_op jit(solution)/shard_map/ppermute | solution.py:356
  107.3 16.6 %collective-permute-start.3 = (bf16[64,2048]{1,0:T(8,128)(2,1)S(1)}, bf16[64,2048]{1,0:T(8,128)(2,1)S(1)}, u32[]{:S(2)}, u32[]{:S(2)}) collective-permute-start(bf16[64,2048]{1,0:T(8,128)(2,1)S(1)} %get-tuple-element.69), channel_id=1, source_target_pairs={{0,8},{1,9},{2,10},{3,11},{4,12},{5,13},{6,14},{7,15},{8,0},{9,1},... | collective-permute-start | bytes 786440 | tf_op jit(solution)/shard_map/ppermute | solution.py:356
  107.3 17.1 %collective-permute-start.4 = (bf16[64,2048]{1,0:T(8,128)(2,1)S(1)}, bf16[64,2048]{1,0:T(8,128)(2,1)S(1)}, u32[]{:S(2)}, u32[]{:S(2)}) collective-permute-start(bf16[64,2048]{1,0:T(8,128)(2,1)S(1)} %get-tuple-element.70), channel_id=1, source_target_pairs={{0,10},{1,11},{2,8},{3,9},{4,14},{5,15},{6,12},{7,13},{8,2},{9,3},... | collective-permute-start | bytes 786440 | tf_op jit(solution)/shard_map/ppermute | solution.py:356
  108.2 19.1 %collective-permute-start.5 = (bf16[64,2048]{1,0:T(8,128)(2,1)S(1)}, bf16[64,2048]{1,0:T(8,128)(2,1)S(1)}, u32[]{:S(2)}, u32[]{:S(2)}) collective-permute-start(bf16[64,2048]{1,0:T(8,128)(2,1)S(1)} %get-tuple-element.71), channel_id=1, source_target_pairs={{0,12},{1,13},{2,14},{3,15},{4,8},{5,9},{6,10},{7,11},{8,4},{9,5},... | collective-permute-start | bytes 786440 | tf_op jit(solution)/shard_map/ppermute | solution.py:356
  110.3 17.4 %collective-permute-start.6 = (bf16[64,2048]{1,0:T(8,128)(2,1)S(1)}, bf16[64,2048]{1,0:T(8,128)(2,1)S(1)}, u32[]{:S(2)}, u32[]{:S(2)}) collective-permute-start(bf16[64,2048]{1,0:T(8,128)(2,1)S(1)} %get-tuple-element.72), channel_id=1, source_target_pairs={{0,14},{1,15},{2,12},{3,13},{4,10},{5,11},{6,8},{7,9},{8,6},{9,7},... | collective-permute-start | bytes 786440 | tf_op jit(solution)/shard_map/ppermute | solution.py:356
  123.8 17.5 %collective-permute-start.34 = (bf16[64,1024]{1,0:T(8,128)(2,1)S(1)}, bf16[64,1024]{1,0:T(8,128)(2,1)S(1)}, u32[]{:S(2)}, u32[]{:S(2)}) collective-permute-start(bf16[64,1024]{1,0:T(8,128)(2,1)S(1)} %get-tuple-element.103), channel_id=1, source_target_pairs={{0,2},{1,3},{2,0},{3,1},{4,6},{5,7},{6,4},{7,5},{8,10},{9,11},{10,... | collective-permute-start | bytes 393224 | tf_op jit(solution)/shard_map/ppermute | solution.py:356
  123.9 18.8 %collective-permute-start.35 = (bf16[64,1024]{1,0:T(8,128)(2,1)S(1)}, bf16[64,1024]{1,0:T(8,128)(2,1)S(1)}, u32[]{:S(2)}, u32[]{:S(2)}) collective-permute-start(bf16[64,1024]{1,0:T(8,128)(2,1)S(1)} %get-tuple-element.104), channel_id=1, source_target_pairs={{0,4},{1,5},{2,6},{3,7},{4,0},{5,1},{6,2},{7,3},{8,12},{9,13},{10,... | collective-permute-start | bytes 393224 | tf_op jit(solution)/shard_map/ppermute | solution.py:356
  124.4 20.8 %collective-permute-start.36 = (bf16[64,1024]{1,0:T(8,128)(2,1)S(1)}, bf16[64,1024]{1,0:T(8,128)(2,1)S(1)}, u32[]{:S(2)}, u32[]{:S(2)}) collective-permute-start(bf16[64,1024]{1,0:T(8,128)(2,1)S(1)} %get-tuple-element.105), channel_id=1, source_target_pairs={{0,6},{1,7},{2,4},{3,5},{4,2},{5,3},{6,0},{7,1},{8,14},{9,15},{10,... | collective-permute-start | bytes 393224 | tf_op jit(solution)/shard_map/ppermute | solution.py:356
  127.3 18.4 %collective-permute-start.37 = (bf16[64,1024]{1,0:T(8,128)(2,1)S(1)}, bf16[64,1024]{1,0:T(8,128)(2,1)S(1)}, u32[]{:S(2)}, u32[]{:S(2)}) collective-permute-start(bf16[64,1024]{1,0:T(8,128)(2,1)S(1)} %get-tuple-element.106), channel_id=1, source_target_pairs={{0,8},{1,9},{2,10},{3,11},{4,12},{5,13},{6,14},{7,15},{8,0},{9,1},... | collective-permute-start | bytes 393224 | tf_op jit(solution)/shard_map/ppermute | solution.py:356
  127.7 18.5 %collective-permute-start.38 = (bf16[64,1024]{1,0:T(8,128)(2,1)S(1)}, bf16[64,1024]{1,0:T(8,128)(2,1)S(1)}, u32[]{:S(2)}, u32[]{:S(2)}) collective-permute-start(bf16[64,1024]{1,0:T(8,128)(2,1)S(1)} %get-tuple-element.107), channel_id=1, source_target_pairs={{0,10},{1,11},{2,8},{3,9},{4,14},{5,15},{6,12},{7,13},{8,2},{9,3},... | collective-permute-start | bytes 393224 | tf_op jit(solution)/shard_map/ppermute | solution.py:356
  153.6 24.4 %collective-permute-start.10 = (bf16[64,2048]{1,0:T(8,128)(2,1)S(1)}, bf16[64,2048]{1,0:T(8,128)(2,1)S(1)}, u32[]{:S(2)}, u32[]{:S(2)}) collective-permute-start(bf16[64,2048]{1,0:T(8,128)(2,1)S(1)} %get-tuple-element.74), channel_id=1, source_target_pairs={{0,2},{1,3},{2,0},{3,1},{4,6},{5,7},{6,4},{7,5},{8,10},{9,11},{10,... | collective-permute-start | bytes 786440 | tf_op jit(solution)/shard_map/ppermute | solution.py:356
  162.9 16.3 %collective-permute-start.11 = (bf16[64,2048]{1,0:T(8,128)(2,1)S(1)}, bf16[64,2048]{1,0:T(8,128)(2,1)S(1)}, u32[]{:S(2)}, u32[]{:S(2)}) collective-permute-start(bf16[64,2048]{1,0:T(8,128)(2,1)S(1)} %get-tuple-element.75), channel_id=1, source_target_pairs={{0,4},{1,5},{2,6},{3,7},{4,0},{5,1},{6,2},{7,3},{8,12},{9,13},{10,... | collective-permute-start | bytes 786440 | tf_op jit(solution)/shard_map/ppermute | solution.py:356
  164.7 15.4 %collective-permute-start.12 = (bf16[64,2048]{1,0:T(8,128)(2,1)S(1)}, bf16[64,2048]{1,0:T(8,128)(2,1)S(1)}, u32[]{:S(2)}, u32[]{:S(2)}) collective-permute-start(bf16[64,2048]{1,0:T(8,128)(2,1)S(1)} %get-tuple-element.76), channel_id=1, source_target_pairs={{0,6},{1,7},{2,4},{3,5},{4,2},{5,3},{6,0},{7,1},{8,14},{9,15},{10,... | collective-permute-start | bytes 786440 | tf_op jit(solution)/shard_map/ppermute | solution.py:356
  169.1 17.9 %collective-permute-start.13 = (bf16[64,2048]{1,0:T(8,128)(2,1)S(1)}, bf16[64,2048]{1,0:T(8,128)(2,1)S(1)}, u32[]{:S(2)}, u32[]{:S(2)}) collective-permute-start(bf16[64,2048]{1,0:T(8,128)(2,1)S(1)} %get-tuple-element.77), channel_id=1, source_target_pairs={{0,8},{1,9},{2,10},{3,11},{4,12},{5,13},{6,14},{7,15},{8,0},{9,1},... | collective-permute-start | bytes 786440 | tf_op jit(solution)/shard_map/ppermute | solution.py:356
  174.1 33.1 %collective-permute-start.41 = (bf16[256,1024]{1,0:T(8,128)(2,1)S(1)}, bf16[256,1024]{1,0:T(8,128)(2,1)S(1)}, u32[]{:S(2)}, u32[]{:S(2)}) collective-permute-start(bf16[256,1024]{1,0:T(8,128)(2,1)S(1)} %mix.4), channel_id=1, source_target_pairs={{0,16},{1,17},{2,18},{3,19},{4,20},{5,21},{6,22},{7,23},{8,24},{9,... | collective-permute-start | bytes 1572872 | tf_op jit(solution)/shard_map/ppermute | solution.py:356
  178.0 29.2 %collective-permute-start.49 = (bf16[256,1024]{1,0:T(8,128)(2,1)S(1)}, bf16[256,1024]{1,0:T(8,128)(2,1)S(1)}, u32[]{:S(2)}, u32[]{:S(2)}) collective-permute-start(bf16[256,1024]{1,0:T(8,128)(2,1)S(1)} %mix.5), channel_id=1, source_target_pairs={{0,16},{1,17},{2,18},{3,19},{4,20},{5,21},{6,22},{7,23},{8,24},{9,... | collective-permute-start | bytes 1572872 | tf_op jit(solution)/shard_map/ppermute | solution.py:356
  179.2 18.9 %collective-permute-start.14 = (bf16[64,2048]{1,0:T(8,128)(2,1)S(1)}, bf16[64,2048]{1,0:T(8,128)(2,1)S(1)}, u32[]{:S(2)}, u32[]{:S(2)}) collective-permute-start(bf16[64,2048]{1,0:T(8,128)(2,1)S(1)} %get-tuple-element.78), channel_id=1, source_target_pairs={{0,10},{1,11},{2,8},{3,9},{4,14},{5,15},{6,12},{7,13},{8,2},{9,3},... | collective-permute-start | bytes 786440 | tf_op jit(solution)/shard_map/ppermute | solution.py:356
  180.1 22.8 %collective-permute-start.15 = (bf16[64,2048]{1,0:T(8,128)(2,1)S(1)}, bf16[64,2048]{1,0:T(8,128)(2,1)S(1)}, u32[]{:S(2)}, u32[]{:S(2)}) collective-permute-start(bf16[64,2048]{1,0:T(8,128)(2,1)S(1)} %get-tuple-element.79), channel_id=1, source_target_pairs={{0,12},{1,13},{2,14},{3,15},{4,8},{5,9},{6,10},{7,11},{8,4},{9,5},... | collective-permute-start | bytes 786440 | tf_op jit(solution)/shard_map/ppermute | solution.py:356
  187.0 18.8 %collective-permute-start.16 = (bf16[64,2048]{1,0:T(8,128)(2,1)S(1)}, bf16[64,2048]{1,0:T(8,128)(2,1)S(1)}, u32[]{:S(2)}, u32[]{:S(2)}) collective-permute-start(bf16[64,2048]{1,0:T(8,128)(2,1)S(1)} %get-tuple-element.80), channel_id=1, source_target_pairs={{0,14},{1,15},{2,12},{3,13},{4,10},{5,11},{6,8},{7,9},{8,6},{9,7},... | collective-permute-start | bytes 786440 | tf_op jit(solution)/shard_map/ppermute | solution.py:356
  (29 other events, 222.8 us)
